TPU v7x, 512 devices: a whole 4x4x16 slice. The times are simulated.
512 devices in a mesh: leaf: 128 (over x_hi, z, y), sub: 4 (over x_lo, core).
Axes of the slice: x: 4 (x_hi: 2, x_lo: 2; x = x_hi * 2 + x_lo), y: 4, z: 16, core: 2. Of those that a mesh axis runs over, the one named last changes fastest.
Arguments:
- points: float32 [16384, 3, 128], P(('leaf', 'sub')), may hold values from 0 to 1
- charges: float32 [16384, 8, 128], P(('leaf', 'sub')), may hold values from -6 to 6
- leaf_skel: float32 [16384, 3, 64], P(('leaf', 'sub')), may hold values from 0 to 1
- mid_skel: float32 [2048, 3, 64], P(('leaf', 'sub')), may hold values from 0 to 1
- root_skel: float32 [128, 3, 64], replicated, may hold values from 0 to 1
- leaf_transfer: float32 [16384, 64, 64], P(('leaf', 'sub')), may hold values from -0.25 to 0.25
- mid_transfer: float32 [2048, 64, 64], P(('leaf', 'sub')), may hold values from -0.75 to 0.75
- near_list: int32 [16384, 27], P(('leaf', 'sub')), may hold values from -1 to 16383, as said below
- far_list: int32 [16384, 20], P(('leaf', 'sub')), may hold values from -1 to 16383, as said below
- mid_list: int32 [2048, 6], P(('leaf', 'sub')), may hold values from -1 to 2047, as said below
- root_list: int32 [128, 6], P('leaf'), may hold values from -1 to 127, as said below
Outputs:
- potentials: float32 [16384, 8, 128], P(('leaf', 'sub'))
Inputs may be any that keep to these rules, and one draw needn't show every extreme that they name: `near_list`: slot 0 of a leaf's row is the leaf itself. Every other entry is -1 or a leaf other than itself that lies on the same device or on one of the two devices beside it in the order of leaf indices; no leaf appears twice in the near and coupling rows of one leaf together. `far_list`: every entry is -1 or a leaf other than the row's own that lies on the same device or on one of the two devices beside it in the order of leaf indices, never one of the row's near_list entries. `mid_list`: every entry is -1 or a middle cluster other than the row's own under the same subtree root, at most once in a row. `root_list`: every entry is -1 or a root other than the row's own, at most once in a row.
All inputs are finite; a program needn't handle non-finite values.
Results may differ from a plain program's by a relative error of at most 0.0003.
Values sent between devices are 32-bit elements; how exact they have to be, the bound alone decides.
A program may use at most 64 MiB of HBM per device.

v0:
```python
import math

import jax
import jax.numpy as jnp
from jax import lax
from jax.sharding import PartitionSpec as P

DELTA2 = 0.0025
EXACT_PRECISION = lax.Precision.HIGHEST


def extended(block, sides, width):
    for axis, dim in sides:
        count = lax.axis_size(axis)
        forward = [(i, i + 1) for i in range(count - 1)]
        backward = [(target, source) for source, target in forward]
        low = lax.ppermute(
            lax.slice_in_dim(block, block.shape[dim] - width, None, axis=dim), axis, forward
        )
        high = lax.ppermute(lax.slice_in_dim(block, 0, width, axis=dim), axis, backward)
        block = jnp.concatenate([low, block, high], axis=dim)
    return block


def kernel(targets, sources):
    first = targets[:, 0, :, None] - sources[:, 0, None, :]
    second = targets[:, 1, :, None] - sources[:, 1, None, :]
    third = targets[:, 2, :, None] - sources[:, 2, None, :]
    return 1.0 / jnp.sqrt(first * first + second * second + third * third + DELTA2)


def lookup(table, partner_idx, offset):
    present = (partner_idx >= 0).astype(jnp.float32)
    position = jnp.clip(partner_idx - offset, 0, table.shape[0] - 1)
    return (table[position], present)


def couple(target_skel, coeff_table, skel_table, lists, offset, nrhs_count, scale):

    def add_slot(slot_no, running):
        partner_idx = lax.dynamic_slice_in_dim(lists, slot_no, 1, 1)[:, 0]
        partner_coeffs, present = lookup(coeff_table, partner_idx, offset)
        partner_skel, unused = lookup(skel_table, partner_idx, offset)
        matrix = kernel(target_skel, partner_skel)
        term = jnp.einsum("lab,lrb->lra", matrix, partner_coeffs, precision=EXACT_PRECISION)
        return running + term * (present * scale)[:, None, None]

    start_value = jnp.zeros((target_skel.shape[0], nrhs_count, coeff_table.shape[2]), jnp.float32)
    return lax.fori_loop(0, lists.shape[1], add_slot, start_value)


def local(
    points,
    charges,
    leaf_skel,
    mid_skel,
    root_skel,
    leaf_transfer,
    mid_transfer,
    near_list,
    far_list,
    mid_list,
    root_list,
):
    leaves = points.shape[0]
    nrhs_count = charges.shape[1]
    rank_count = leaf_skel.shape[2]
    leaf_count = points.shape[2]
    leaf_scale = 1.0 / math.sqrt(leaf_count)
    rank_scale = 1.0 / rank_count
    flat_index = lax.axis_index(("leaf", "sub"))
    window_start = (flat_index - 1) * leaves
    packed_points = jnp.concatenate([points, charges], axis=1)
    widened = extended(packed_points, ((("leaf", "sub"), 0),), leaves)

    def add_near(slot_no, running):
        partner_idx = lax.dynamic_slice_in_dim(near_list, slot_no, 1, 1)[:, 0]
        partner_rows, present = lookup(widened, partner_idx, window_start)
        matrix = kernel(points, partner_rows[:, :3])
        term = jnp.einsum("lpq,lrq->lrp", matrix, partner_rows[:, 3:], precision=EXACT_PRECISION)
        return running + term * (present / leaf_count)[:, None, None]

    near = lax.fori_loop(0, near_list.shape[1], add_near, jnp.zeros(charges.shape, jnp.float32))
    basis = kernel(points, leaf_skel)
    expansion_weights = (
        jnp.einsum("lpa,lrp->lra", basis, charges, precision=EXACT_PRECISION) * leaf_scale
    )
    packed_coeffs = jnp.concatenate([expansion_weights, leaf_skel], axis=1)
    fine_table = extended(packed_coeffs, ((("leaf", "sub"), 0),), leaves)
    leaf_potential_field = couple(
        leaf_skel,
        fine_table[:, :nrhs_count],
        fine_table[:, nrhs_count:],
        far_list,
        window_start,
        nrhs_count,
        rank_scale,
    )
    mids = leaves // 8
    leaf_cluster_groups = leaf_transfer.reshape(mids, 8, rank_count, rank_count)
    middle_expansion_weights = jnp.einsum(
        "hpsi,hpds->hdi",
        leaf_cluster_groups,
        expansion_weights.reshape(mids, 8, nrhs_count, rank_count),
        precision=EXACT_PRECISION,
    )
    packed_mid = jnp.concatenate([middle_expansion_weights, mid_skel], axis=1)
    mid_table = lax.all_gather(packed_mid, "sub", axis=0, tiled=True)
    group_start = lax.axis_index("leaf") * mid_table.shape[0]
    mid_field = couple(
        mid_skel,
        mid_table[:, :nrhs_count],
        mid_table[:, nrhs_count:],
        mid_list,
        group_start,
        nrhs_count,
        rank_scale,
    )
    partial_root = jnp.einsum(
        "mab,mra->rb", mid_transfer, middle_expansion_weights, precision=EXACT_PRECISION
    )
    summed_root = lax.psum(partial_root, "sub")
    root_table = lax.all_gather(summed_root[None], "leaf", axis=0, tiled=True)
    root_number = lax.axis_index("leaf")
    my_skel = lax.dynamic_slice_in_dim(root_skel, root_number, 1, 0)
    root_field = couple(my_skel, root_table, root_skel, root_list, 0, nrhs_count, rank_scale)
    middle_potential_total = mid_field + jnp.einsum(
        "mab,rb->mra", mid_transfer, root_field[0], precision=EXACT_PRECISION
    )
    leaf_potential_total = leaf_potential_field + jnp.einsum(
        "oxgc,osc->oxsg", leaf_cluster_groups, middle_potential_total, precision=EXACT_PRECISION
    ).reshape(leaves, nrhs_count, rank_count)
    return (
        near
        + jnp.einsum("lpa,lra->lrp", basis, leaf_potential_total, precision=EXACT_PRECISION)
        * leaf_scale
    )


def solution(mesh):
    in_specs = (
        P(("leaf", "sub"), None, None),
        P(("leaf", "sub"), None, None),
        P(("leaf", "sub"), None, None),
        P(("leaf", "sub"), None, None),
        P(),
        P(("leaf", "sub"), None, None),
        P(("leaf", "sub"), None, None),
        P(("leaf", "sub"), None),
        P(("leaf", "sub"), None),
        P(("leaf", "sub"), None),
        P("leaf", None),
    )
    out_specs = P(("leaf", "sub"), None, None)
    return jax.shard_map(local, mesh=mesh, in_specs=in_specs, out_specs=out_specs, check_vma=False)
```

profile of v0, /device:TPU:2, one launch (start us, length us, event | category | flops | bytes accessed | tf_op | source)
XLA Modules:
  0.0 699.5 jit_solution(9708654243711353516)
XLA Ops:
  2.5 3.5 convolution_multiply_fusion.4
  7.9 3.6 collective-permute-start.3
  13.6 5.6 collective-permute-start.1
  19.9 5.4 all_gather.6
  25.4 10.1 %while.60 = (s32[]{:T(128)}, f32[4,8,64]{2,1,0:T(8,128)S(1)}, s32[4,6]{0,1:T(8,128)S(1)}, s32[]{:T(128)}, f32[16,8,64]{2,1,0:T(8,128)S(1)}, /*index=5*/f32[4,3,6...) while((s32[]{:T(128)}, f32[4,8,64]{2,1,0:T(8,128)S(1)}, s32[4,6]{0,1:T(8,128)S(1)}, ...), condition=%wide.region_5.6_spmd.clone, body=%wide.region_4.5_spmd.clone.sunk | while | flops 1727519 | bytes 69875 | solution.py:49
  35.8 7.4 %psum.7 = f32[1,8,64]{2,1,0:T(8,128)S(1)} all-reduce(f32[1,8,64]{2,1,0:T(8,128)S(1)} %convolution_bitcast_fusion.2), channel_id=1, replica_groups=mesh['leaf'=128,'sub'=4] {'sub'}, use_global_device_ids=true, to_apply=%region_6.7 | all-reduce | flops 512 | bytes 4096 | tf_op jit(solution)/shard_map/psum | solution.py:122
  43.2 364.2 %all_gather.7 = f32[128,8,64]{2,1,0:T(8,128)S(1)} all-gather(f32[1,8,64]{2,1,0:T(8,128)S(1)} %psum.7), channel_id=1, replica_groups=mesh['leaf'=128,'sub'=4] {'leaf'}, dimensions={0}, use_global_device_ids=true | all-gather | bytes 264192 | tf_op jit(solution)/shard_map/all_gather | solution.py:123
  407.6 12.6 %while.61 = (s32[]{:T(128)}, f32[1,8,64]{2,1,0:T(8,128)S(1)}, s32[1,6]{1,0:T(1,128)S(1)}, f32[128,8,64]{2,1,0:T(8,128)S(1)}, f32[1,3,64]{2,1,0:T(4,128)S(1)}, /*...) while((s32[]{:T(128)}, f32[1,8,64]{2,1,0:T(8,128)S(1)}, ...), condition=%wide.region_8.9_spmd.clone, body=%wide.region_7.8_spmd.clone.sunk | while | flops 431623 | bytes 18109 | solution.py:49
  425.1 113.0 %while.59 = (s32[]{:T(128)}, f32[32,8,64]{2,1,0:T(8,128)S(1)}, s32[32,20]{0,1:T(8,128)}, s32[]{:T(128)}, f32[96,8,64]{2,1,0:T(8,128)S(1)}, /*index=5*/f32[32,3,6...) while((s32[]{:T(128)}, f32[32,8,64]{2,1,0:T(8,128)S(1)}, s32[32,20]{0,1:T(8,128)}, ...), condition=%wide.region_3.4_spmd.clone, body=%wide.region_2.3_spmd.clone.sunk | while | flops 13812963 | bytes 529523 | solution.py:49
  427.7 3.0 fusion.162
  439.1 3.0 fusion.162
  444.7 3.0 fusion.162
  450.4 3.0 fusion.162
  473.0 3.0 fusion.162
  478.6 3.0 fusion.162
  484.3 3.0 fusion.162
  495.6 3.0 fusion.162
  501.2 3.0 fusion.162
  506.9 3.0 fusion.162
  512.5 3.0 fusion.162
  541.2 157.6 %while.58 = (s32[]{:T(128)}, f32[32,8,128]{2,1,0:T(8,128)S(1)}, s32[32,27]{0,1:T(8,128)S(1)}, s32[]{:T(128)}, f32[96,11,128]{2,1,0:T(8,128)S(1)}, /*index=5*/f32[32,3,128]{2,0,1:T(8,128)S(1)}, s32[]{:T(128)}, s32[]{:T(128)}) while((s32[]{:T(128)}, f32[32,8,128]{2,1,0:T(8,128)S(1)}, s32[32,27]{0,1:T(8,128)S(1)}, s32[]{:T(128)}, ...), condition=%wide.region_1.2_spmd.clone, body=%wide.region_0.1_spmd.clone.sunk | while | flops 55149792 | bytes 1054059 | solution.py:83
  542.0 5.1 fusion.156
  547.8 5.1 fusion.156
  553.6 5.1 fusion.156
  559.5 5.1 fusion.156
  565.3 5.1 fusion.156
  571.1 5.1 fusion.156
  577.0 5.1 fusion.156
  582.8 5.1 fusion.156
  588.7 5.1 fusion.156
  594.5 5.1 fusion.156
  600.3 5.1 fusion.156
  606.2 5.1 fusion.156
  612.0 5.1 fusion.156
  617.8 5.1 fusion.156
  623.7 5.1 fusion.156
  629.5 5.1 fusion.156
  635.4 5.1 fusion.156
  641.2 5.1 fusion.156
  647.0 5.1 fusion.156
  652.9 5.1 fusion.156
  658.7 5.1 fusion.156
  664.5 5.1 fusion.156
  670.4 5.1 fusion.156
  676.2 5.1 fusion.156
  682.0 5.1 fusion.156
  687.9 5.1 fusion.156
  693.7 5.1 fusion.156
  (455 shorter events, 128.4 us)
Async XLA Ops:
  0.0 19.2 %copy-start = (f32[32,64,64]{2,1,0:T(8,128)S(1)}, f32[32,64,64]{2,1,0:T(8,128)}, u32[]{:S(2)}) copy-start(f32[32,64,64]{2,1,0:T(8,128)} %param.24) | copy-start | bytes 1572868
  2.4 3.5 copy-start.10
  2.4 3.5 copy-start.12
  2.4 9.2 %copy-start.2 = (f32[32,3,128]{2,0,1:T(8,128)S(1)}, f32[32,3,128]{2,0,1:T(8,128)}, u32[]{:S(2)}) copy-start(f32[32,3,128]{2,0,1:T(8,128)} %param.19) | copy-start | bytes 147460
  2.5 9.2 %copy-start.3 = (f32[32,8,128]{2,1,0:T(8,128)S(1)}, f32[32,8,128]{2,1,0:T(8,128)}, u32[]{:S(2)}) copy-start(f32[32,8,128]{2,1,0:T(8,128)} %param.20) | copy-start | bytes 393220
  2.5 16.7 %copy-start.5 = (f32[4,3,64]{2,0,1:T(4,128)S(1)}, f32[4,3,64]{2,0,1:T(4,128)}, u32[]{:S(2)}) copy-start(f32[4,3,64]{2,0,1:T(4,128)} %param.22) | copy-start | bytes 9220
  6.0 417.5 %collective-permute-start.2 = (f32[32,11,64]{2,1,0:T(8,128)S(1)}, f32[32,11,64]{2,1,0:T(8,128)S(1)}, u32[]{:S(2)}, u32[]{:S(2)}) collective-permute-start(f32[32,11,64]{2,1,0:T(8,128)S(1)} %pad_maximum_fusion.3), channel_id=1, source_target_pairs={{0,1},{1,2},{2,3},{3,4},{4,5},{5,6},{6,7},{7,8},{8,9},{9,10},{10,1... | collective-permute-start | bytes 270344 | tf_op jit(solution)/shard_map/ppermute | solution.py:17
  7.9 415.7 %collective-permute-start.3 = (f32[32,11,64]{2,1,0:T(8,128)S(1)}, f32[32,11,64]{2,1,0:T(8,128)S(1)}, u32[]{:S(2)}, u32[]{:S(2)}) collective-permute-start(f32[32,11,64]{2,1,0:T(8,128)S(1)} %pad_maximum_fusion.3), channel_id=1, source_target_pairs={{1,0},{2,1},{3,2},{4,3},{5,4},{6,5},{7,6},{8,7},{9,8},{10,9},{11,1... | collective-permute-start | bytes 270344 | tf_op jit(solution)/shard_map/ppermute | solution.py:20
  11.7 13.7 %copy-start.15 = (s32[4,6]{1,0:T(4,128)S(1)}, s32[4,6]{1,0:T(4,128)}, u32[]{:S(2)}) copy-start(s32[4,6]{1,0:T(4,128)} %param.28) | copy-start | bytes 292
  11.7 528.4 %collective-permute-start = (f32[32,11,128]{2,1,0:T(8,128)S(1)}, f32[32,11,128]{2,1,0:T(8,128)}, u32[]{:S(2)}, u32[]{:S(2)}) collective-permute-start(f32[32,11,128]{2,1,0:T(8,128)S(1)} %pad_maximum_fusion.2), channel_id=1, source_target_pairs={{0,1},{1,2},{2,3},{3,4},{4,5},{5,6},{6,7},{7,8},{8,9},{9,10},{10,1... | collective-permute-start | bytes 540680 | tf_op jit(solution)/shard_map/ppermute | solution.py:17
  13.6 526.5 %collective-permute-start.1 = (f32[32,11,128]{2,1,0:T(8,128)S(1)}, f32[32,11,128]{2,1,0:T(8,128)}, u32[]{:S(2)}, u32[]{:S(2)}) collective-permute-start(f32[32,11,128]{2,1,0:T(8,128)S(1)} %pad_maximum_fusion.2), channel_id=1, source_target_pairs={{1,0},{2,1},{3,2},{4,3},{5,4},{6,5},{7,6},{8,7},{9,8},{10,9},{11,1... | collective-permute-start | bytes 540680 | tf_op jit(solution)/shard_map/ppermute | solution.py:20
  25.4 10.1 %copy-start.4 = (f32[4,64,64]{2,1,0:T(8,128)S(1)}, f32[4,64,64]{2,1,0:T(8,128)}, u32[]{:S(2)}) copy-start(f32[4,64,64]{2,1,0:T(8,128)} %param.25) | copy-start | bytes 196612
  25.4 382.0 %copy-start.8 = (f32[128,3,64]{0,2,1:T(8,128)S(1)}, f32[128,3,64]{0,2,1:T(8,128)}, u32[]{:S(2)}) copy-start(f32[128,3,64]{0,2,1:T(8,128)} %param.23) | copy-start | bytes 294916
  35.5 372.0 %copy-start.14 = (s32[1,6]{1,0:T(1,128)S(1)}, s32[1,6]{1,0:T(1,128)}, u32[]{:S(2)}) copy-start(s32[1,6]{1,0:T(1,128)} %param.29) | copy-start | bytes 76
  420.2 3.2 copy-start.9
  424.1 0.8 copy-start.1
  424.1 0.9 copy-start.7
  425.1 113.1 %copy-start.11 = (f32[32,128]{1,0:T(8,128)S(1)}, f32[32,128]{1,0:T(8,128)}, u32[]{:S(2)}) copy-start(f32[32,128]{1,0:T(8,128)} %copy-done.10) | copy-start | bytes 49156
  425.1 113.1 %copy-start.13 = (f32[32,128]{1,0:T(8,128)S(1)}, f32[32,128]{1,0:T(8,128)}, u32[]{:S(2)}) copy-start(f32[32,128]{1,0:T(8,128)} %copy-done.12) | copy-start | bytes 49156
  540.1 1.2 copy-start.6
where the time goes:
time: 703 us; the launch traced here: 700 us
  blocking collectives  377 us (54%)
  matrix products  211 us (30%)
  local copies, waits for them, and re-layouts  52.6 us (7%)
  other arithmetic  35.4 us (5%)
  starting transfers between devices  13 us (2%)
  loops' own time  10.1 us (1%)
    all_gather x1, blocking collectives, local(): root_table = lax.all_gather(summed_root[None], 'leaf', axis=0, tiled=True)  364 us
    dot_general x27, matrix products, add_near(): jnp.einsum('lpq,lrq->lrp', matrix, partner_rows[:, 3:], precision=EXACT_P...  138 us
    dot_general x32, matrix products, add_slot(): jnp.einsum('lab,lrb->lra', matrix, partner_coeffs, precision=EXACT_PRECIS...  63.4 us
    gather x85, local copies, waits for them, and re-layouts, lookup(): return (table[position], present)  46.4 us
    select_n x53, other arithmetic, lookup(): return (table[position], present)  14.7 us
  transfers between devices with their start and end apart: 4, of which 0 were waited for; matrix products, arithmetic and copies ran while one was open for 19% of the time, Pallas kernels for 0%

commit v1 on v0

v1 whole, which is shorter than its diff:
```python
import functools
import math

import jax
import jax.numpy as jnp
from jax import lax
from jax.experimental import pallas as pl
from jax.experimental.pallas import tpu as pltpu
from jax.sharding import PartitionSpec as P

DELTA2 = 0.0025
MESH = pl.DeviceIdType.MESH
BF = jnp.bfloat16
F32 = jnp.float32
TN = (((0,), (1,)), ((), ()))
TT = (((0,), (0,)), ((), ()))
NT = (((1,), (1,)), ((), ()))
YS, ZS, XS, SUBS = 4, 16, 2, 4


def rows_of(x):
    return lax.broadcasted_iota(jnp.int32, x.shape, 0)


def low_half(shape):
    return lax.broadcasted_iota(jnp.int32, shape, len(shape) - 1) < 64


def split2(x):
    high = x.astype(BF)
    return high, (x - high.astype(F32)).astype(BF)


def stacked(x):
    high = x.astype(BF).astype(F32)
    return jnp.concatenate([high, x - high], axis=0).astype(BF)


def split3(x):
    first = x.astype(BF).astype(F32)
    rest = x - first
    second = rest.astype(BF).astype(F32)
    return first, second, (rest - second).astype(BF).astype(F32)


def centred(p):
    c = p - 0.5
    return jnp.concatenate([c, jnp.sum(c * c, axis=0, keepdims=True) + 0.5 * DELTA2], axis=0)


def doubled(s):
    return jnp.concatenate([s, s], axis=1)


def source_rows(p8):
    p1, p2, p3 = split3(p8)
    norm = (rows_of(p8) & 3) == 3
    ones = jnp.where(norm, 1.0, p1)
    return jnp.concatenate([p1, p2, p3, ones, jnp.where(norm, 1.0, p2), ones], axis=0).astype(BF)


def target_rows(p8, first_half):
    p1, p2, p3 = split3(p8)
    row = rows_of(p8)
    norm = (row & 3) == 3
    active = ((row < 4) if first_half else (row >= 4)).astype(F32)
    lead = jnp.where(norm, 1.0, -2.0 * p1) * active
    return jnp.concatenate(
        [
            lead,
            lead,
            lead,
            jnp.where(norm, p1, -2.0 * p2) * active,
            jnp.where(norm, p2, -2.0 * p2) * active,
            jnp.where(norm, p3, -2.0 * p3) * active,
        ],
        axis=0,
    )


def split_dot(two, matrix, dims):
    high, low = split2(matrix)
    out = lax.dot_general(two, high, dims, preferred_element_type=F32) + lax.dot_general(
        two, low, dims, preferred_element_type=F32
    )
    half = out.shape[0] // 2
    return out[:half] + out[half:]


NN = (((1,), (0,)), ((), ()))


def upward(
    points, charges, leaf_skel, mid_skel, leaf_transfer, mid_transfer,
    win, cwin, mids, roots, rpart, yroots, send, recv,
):
    leaf, sub = lax.axis_index("leaf"), lax.axis_index("sub")
    leaves = points.shape[0]
    nleaf = XS * ZS * YS
    flat = leaf * SUBS + sub
    total = nleaf * SUBS
    x, z, y = leaf // (ZS * YS), (leaf // YS) % ZS, leaf % YS
    right, left = (flat + 1) % total, (flat + total - 1) % total
    right_id, left_id = (right // SUBS, right % SUBS), (left // SUBS, left % SUBS)
    sub_ids = [(leaf, (sub + k) % SUBS) for k in range(1, SUBS)]
    y_ids = [(leaf - y + (y + k) % YS, sub) for k in range(1, YS)]
    z_ids = [((x * ZS + (z + k) % ZS) * YS + y, sub) for k in range(1, ZS)]
    x_id = (((1 - x) * ZS + z) * YS + y, sub)

    barrier = pltpu.get_barrier_semaphore()
    partners = [right_id, left_id] + sub_ids + y_ids + z_ids + [x_id]
    for partner in partners:
        pl.semaphore_signal(barrier, inc=1, device_id=partner, device_id_type=MESH)

    def copy(slot, src, dst, target):
        return pltpu.make_async_remote_copy(
            src_ref=src, dst_ref=dst, send_sem=send.at[slot], recv_sem=recv.at[slot],
            device_id=target, device_id_type=MESH,
        )

    leaf_scale = 1.0 / math.sqrt(points.shape[2])

    def one_leaf(i, carry):
        own = centred(points[i])
        skel = centred(doubled(leaf_skel[i]))
        x_i = charges[i]
        win[leaves + i] = jnp.concatenate([own, skel, x_i], axis=0)
        src = source_rows(jnp.concatenate([own, skel], axis=0))
        tgt = target_rows(jnp.concatenate([skel, skel], axis=0), True).astype(BF)
        d2 = lax.dot_general(src, tgt, TT, preferred_element_type=F32)
        cwin[leaves + i] = split_dot(stacked(x_i), lax.rsqrt(d2), NN) * leaf_scale
        return carry

    lax.fori_loop(0, leaves, one_leaf, 0, unroll=4)

    half = low_half((8, 128))

    def lifted(low_child, high_child, pair):
        both = jnp.where(half, low_child, high_child)
        matrix = pair.reshape(128, 64)
        return split_dot(stacked(both), doubled(matrix), NN)

    my_mids = mid_skel.shape[0]
    mid_coeffs = []
    for m in range(my_mids):
        acc = jnp.zeros((8, 128), F32)
        for k in range(0, 8, 2):
            c = m * 8 + k
            acc += lifted(cwin[leaves + c], cwin[leaves + c + 1], leaf_transfer[c : c + 2])
        mid_coeffs.append(acc)
        skel = centred(doubled(mid_skel[m]))
        mids[sub * my_mids + m] = jnp.concatenate([acc, skel, skel], axis=0)
    partial = jnp.zeros((8, 128), F32)
    for m in range(0, my_mids, 2):
        partial += lifted(mid_coeffs[m], mid_coeffs[m + 1], mid_transfer[m : m + 2])
    rpart[sub] = partial

    pl.semaphore_wait(barrier, len(partners))
    sums = [copy(k, rpart.at[sub], rpart.at[sub], sub_ids[k]) for k in range(3)]
    own_mids = mids.at[pl.ds(sub * my_mids, my_mids)]
    others = [copy(3 + k, own_mids, own_mids, sub_ids[k]) for k in range(3)]
    for n, ref in ((6, win), (8, cwin)):
        own = ref.at[pl.ds(leaves, leaves)]
        others.append(copy(n, own, ref.at[pl.ds(0, leaves)], right_id))
        others.append(copy(n + 1, own, ref.at[pl.ds(2 * leaves, leaves)], left_id))
    for c in sums + others:
        c.start()
    for c in sums:
        c.wait()
    yroots[y] = (rpart[0] + rpart[1]) + (rpart[2] + rpart[3])
    stage = [copy(10 + k, yroots.at[y], yroots.at[y], y_ids[k]) for k in range(YS - 1)]
    for c in stage:
        c.start()
    for c in stage:
        c.wait()
    roots[x, z, 0] = jnp.where(half, yroots[0], yroots[1])
    roots[x, z, 1] = jnp.where(half, yroots[2], yroots[3])
    own = roots.at[x, z]
    stage = [copy(13 + k, own, own, z_ids[k]) for k in range(ZS - 1)]
    for c in stage:
        c.start()
    for c in stage:
        c.wait()
    last = copy(28, roots.at[x], roots.at[x], x_id)
    last.start()
    for c in others:
        c.wait()
    last.wait()


def downward(
    near_list, far_list, mid_list, root_list,
    win, cwin, mids, roots, root_skel, leaf_transfer, mid_transfer,
    out, src, chg, cof, fin, msrc, mcof, rsrc, rcof,
):
    leaf, sub = lax.axis_index("leaf"), lax.axis_index("sub")
    leaves = leaf_transfer.shape[0]
    my_mids = mid_transfer.shape[0]
    window = 3 * leaves
    group = SUBS * my_mids
    start = (leaf * SUBS + sub - 1) * leaves
    rank_scale = 1.0 / leaf_transfer.shape[1]
    zero = jnp.zeros((16, 128), BF)
    half = low_half((8, 128))
    lane48 = low_half((48, 128))
    lane16 = low_half((16, 128))

    def build(j, carry):
        w = win[j]
        src[j] = source_rows(w[:8])
        chg[j] = stacked(w[8:])
        cof[j] = stacked(cwin[j])
        return carry

    lax.fori_loop(0, window, build, 0, unroll=4)
    src[window] = src[0]
    chg[window] = zero
    cof[window] = zero
    for j in range(group):
        w = mids[j]
        msrc[j] = source_rows(w[8:])
        mcof[j] = stacked(w[:8])
    msrc[group] = msrc[0]
    mcof[group] = zero

    def root_p8(r):
        p4 = centred(doubled(root_skel[r]))
        return jnp.concatenate([p4, p4], axis=0)

    slots = root_list.shape[1]
    for k in range(slots):
        r = root_list[0, k]
        present = (r >= 0).astype(F32)
        r = jnp.maximum(r, 0)
        tile = roots[r // 2]
        mine = (lax.broadcasted_iota(jnp.int32, (8, 128), 1) // 64) == (r % 2)
        coeff = jnp.where(mine, tile, pltpu.roll(tile, 64, 1))
        rsrc[k] = source_rows(root_p8(r))
        rcof[k] = stacked(coeff * present)
    for k in range(slots, 8):
        rsrc[k] = rsrc[0]
        rcof[k] = zero

    def far_targets(p8):
        rows = target_rows(p8, False)
        low = low_half(rows.shape)
        pair = jnp.concatenate([jnp.where(low, rows, 0.0), jnp.where(low, 0.0, rows)], axis=0)
        return pair.T.astype(BF)

    def quad(js, table, coeffs, tgt):
        a, b, c, d = js
        s = jnp.concatenate(
            [jnp.where(lane48, table[a], table[c]), jnp.where(lane48, table[b], table[d])], axis=0
        )
        x = jnp.concatenate(
            [jnp.where(lane16, coeffs[a], coeffs[c]), jnp.where(lane16, coeffs[b], coeffs[d])],
            axis=0,
        )
        high, low = split2(lax.rsqrt(lax.dot_general(s, tgt, TN, preferred_element_type=F32)))
        return jnp.dot(x, high, preferred_element_type=F32) + jnp.dot(
            x, low, preferred_element_type=F32
        )

    def field(acc):
        s = jnp.where(half, acc[0:8] + acc[8:16], acc[16:24] + acc[24:32])
        return (s + pltpu.roll(s, 64, 1)) * rank_scale

    acc = quad((0, 1, 2, 3), rsrc, rcof, far_targets(root_p8(leaf)))
    acc += quad((4, 5, 6, 7), rsrc, rcof, far_targets(root_p8(leaf)))
    root_two = stacked(field(acc))[:, :64]

    def lowered(two, matrix):
        return split_dot(two, jnp.concatenate([matrix, matrix], axis=0), NT)

    def place(j, first, empty):
        return jnp.where(j >= 0, j - first, empty)

    mid_two = []
    for m in range(my_mids):
        js = [place(mid_list[m, k], leaf * group, group) for k in range(mid_list.shape[1])]
        js += [group] * (8 - len(js))
        tgt = far_targets(mids[sub * my_mids + m][8:])
        f = field(quad(js[:4], msrc, mcof, tgt) + quad(js[4:], msrc, mcof, tgt))
        mid_two.append(stacked(f + lowered(root_two, mid_transfer[m]))[:, :64])

    up = 0.5 * math.sqrt(128.0)
    for m in range(my_mids):

        def far_leaves(t, carry, m=m):
            for p in range(4):
                i = m * 8 + t * 4 + p
                tgt = far_targets(win[leaves + i][:8])
                acc = jnp.zeros((32, 128), F32)
                for g in range(0, far_list.shape[1], 4):
                    js = [place(far_list[i, g + k], start, window) for k in range(4)]
                    acc += quad(js, src, cof, tgt)
                fin[i] = stacked((field(acc) + lowered(mid_two[m], leaf_transfer[i])) * up)
            return carry

        lax.fori_loop(0, 2, far_leaves, 0)

    def near_leaves(t, carry):
        ids = [t * 4 + p for p in range(4)]
        rows = [win[leaves + i][:8] for i in ids]
        tgts = [target_rows(r, True).T.astype(BF) for r in rows]
        accs = [jnp.zeros((16, 128), F32)] * 4
        count = near_list.shape[1]
        for g in range(0, count, 2):
            for p, i in enumerate(ids):
                j = place(near_list[i, g], start, window)
                if g + 1 < count:
                    k = place(near_list[i, g + 1], start, window)
                    s = jnp.concatenate([src[j], src[k]], axis=1)
                    d2 = lax.dot_general(s, tgts[p], TN, preferred_element_type=F32)
                    x = jnp.concatenate([chg[j], chg[k]], axis=1)
                else:
                    own = jnp.concatenate([rows[p][:4], rows[p][:4]], axis=0)
                    basis = target_rows(own, False).T.astype(BF)
                    d2 = jnp.concatenate(
                        [
                            lax.dot_general(src[j], tgts[p], TN, preferred_element_type=F32),
                            lax.dot_general(
                                src[leaves + i], basis, TN, preferred_element_type=F32
                            ),
                        ],
                        axis=0,
                    )
                    x = jnp.concatenate([chg[j], fin[i]], axis=1)
                high, low = split2(lax.rsqrt(d2))
                accs[p] += jnp.dot(x, high, preferred_element_type=F32) + jnp.dot(
                    x, low, preferred_element_type=F32
                )
        for p, i in enumerate(ids):
            out[i] = (accs[p][:8] + accs[p][8:]) * (1.0 / 128.0)
        return carry

    lax.fori_loop(0, leaves // 4, near_leaves, 0)


def local(
    points, charges, leaf_skel, mid_skel, root_skel, leaf_transfer, mid_transfer,
    near_list, far_list, mid_list, root_list,
):
    leaves = points.shape[0]
    mids = mid_skel.shape[0]
    vmem = pl.BlockSpec(memory_space=pltpu.VMEM)
    smem = pl.BlockSpec(memory_space=pltpu.SMEM)
    shape = jax.ShapeDtypeStruct
    win, cwin, mid_table, roots = pl.pallas_call(
        upward,
        name="upward",
        out_shape=(
            shape((3 * leaves, 16, 128), F32),
            shape((3 * leaves, 8, 128), F32),
            shape((SUBS * mids, 16, 128), F32),
            shape((XS, ZS, YS // 2, 8, 128), F32),
        ),
        in_specs=[vmem] * 6,
        out_specs=(vmem,) * 4,
        scratch_shapes=[
            pltpu.VMEM((SUBS, 8, 128), F32),
            pltpu.VMEM((YS, 8, 128), F32),
            pltpu.SemaphoreType.DMA((29,)),
            pltpu.SemaphoreType.DMA((29,)),
        ],
        compiler_params=pltpu.CompilerParams(collective_id=0, has_side_effects=True),
    )(points, charges, leaf_skel, mid_skel, leaf_transfer, mid_transfer)
    window = 3 * leaves + 1
    group = SUBS * mids + 1
    return pl.pallas_call(
        downward,
        name="downward",
        out_shape=shape((leaves, 8, 128), F32),
        in_specs=[smem] * 4 + [vmem] * 7,
        out_specs=vmem,
        scratch_shapes=[
            pltpu.VMEM((window, 48, 128), BF),
            pltpu.VMEM((window, 16, 128), BF),
            pltpu.VMEM((window, 16, 128), BF),
            pltpu.VMEM((leaves, 16, 128), BF),
            pltpu.VMEM((group, 48, 128), BF),
            pltpu.VMEM((group, 16, 128), BF),
            pltpu.VMEM((8, 48, 128), BF),
            pltpu.VMEM((8, 16, 128), BF),
        ],
    )(
        near_list, far_list, mid_list, root_list,
        win, cwin, mid_table, roots.reshape(XS * ZS * YS // 2, 8, 128),
        root_skel, leaf_transfer, mid_transfer,
    )


def solution(mesh):
    both = P(("leaf", "sub"), None, None)
    lists = P(("leaf", "sub"), None)
    in_specs = (both, both, both, both, P(), both, both, lists, lists, lists, P("leaf", None))
    return jax.shard_map(local, mesh=mesh, in_specs=in_specs, out_specs=both, check_vma=False)
```

time: 703 us -> 90.5 us (0.13)
  the two profiles are of different devices: /device:TPU:2 before, /device:TPU:8 now
where the time goes in v1:
time: 90.5 us; the launch traced here: 90.3 us
  Pallas kernels  85.9 us (95%)
  local copies, waits for them, and re-layouts  4.29 us (5%)
    pallas_call x1, Pallas kernels, local(): pl.pallas_call(upward, name='upward', out_shape=(shape((3 * leaves, 16, 1...  45 us
    pallas_call x1, Pallas kernels, local(): pl.pallas_call(downward, name='downward', out_shape=shape((leaves, 8, 128...  40.9 us
    unnamed x13, local copies, waits for them, and re-layouts  4.29 us

profile of v1, /device:TPU:8, one launch (start us, length us, event | category | flops | bytes accessed | tf_op | source)
XLA Modules:
  0.0 90.3 jit_solution(3054236262816647867)
XLA Ops:
  0.0 0.0 copy-start.1
  0.0 1.5 %copy.12.points = f32[32,3,128]{2,1,0:T(4,128)} copy(f32[32,3,128]{2,0,1:T(8,128)} %param.11) | data formatting | bytes 98304 | tf_op args[0]
  1.5 0.0 copy-done.1
  1.5 0.0 copy-start.3
  1.5 0.7 copy.13.leaf_skel
  2.1 0.0 copy-done.3
  2.2 0.6 copy.14.mid_skel
  2.8 0.0 copy-start
  2.8 45.0 %upward.1 = (f32[96,16,128]{2,1,0:T(8,128)}, f32[96,8,128]{2,1,0:T(8,128)}, f32[16,16,128]{2,1,0:T(8,128)}, f32[2,16,2,8,128]{4,3,2,1,0:T(8,128)}) custom-call(f32[32,3,128]{2,1,0:T(4,128)} %copy.12.points, f32[32,8,128]{2,1,0:T(8,128)} %charges.1, f32[32,3,64]{2,1,0:T(4,128)} %copy.13.leaf_skel, f32[4,3,64]{2,1,0:T(4,128)} %copy.14.mid_skel, ...), custom_call_target="tpu_custom_call" | custom-call | tf_op jit(solution)/shard_map/upward/pallas_call | solution.py:349
  47.8 0.0 copy-done
  47.8 0.0 copy-start.2
  47.8 0.8 copy.16.root_skel
  48.6 0.0 copy-done.2
  48.6 0.7 copy.15.far_list
  49.3 40.9 %downward.1 = f32[32,8,128]{2,1,0:T(8,128)} custom-call(s32[32,27]{1,0:T(8,128)} %near_list.1, s32[32,20]{1,0:T(8,128)} %copy.15.far_list, s32[4,6]{1,0:T(4,128)} %mid_list.1, s32[1,6]{1,0:T(1,128)} %root_list.1, f32[96,16,128]{2,1,0:T(8,128)} %get-tuple-element.9.win, f32[96,8,128]{2,1,0:T(8,128)} %get-tuple-element.10.cwin, ...), custom_call_target="tpu_custom_call" | custom-call | tf_op jit(solution)/shard_map/downward/pallas_call | solution.py:370
Async XLA Ops:
  0.0 1.5 %copy-start.1 = (f32[32,3,64]{2,0,1:T(8,128)S(1)}, f32[32,3,64]{2,0,1:T(8,128)}, u32[]{:S(2)}) copy-start(f32[32,3,64]{2,0,1:T(8,128)} %param.13) | copy-start | bytes 73732
  1.5 0.7 copy-start.3
  2.8 45.0 %copy-start = (f32[128,3,64]{0,2,1:T(8,128)S(1)}, f32[128,3,64]{0,2,1:T(8,128)}, u32[]{:S(2)}) copy-start(f32[128,3,64]{0,2,1:T(8,128)} %param.15) | copy-start | bytes 294916
  47.8 0.9 copy-start.2

commit v2 on v1

v2 whole, which is shorter than its diff:
```python
import functools
import math

import jax
import jax.numpy as jnp
from jax import lax
from jax.experimental import pallas as pl
from jax.experimental.pallas import tpu as pltpu
from jax.sharding import PartitionSpec as P

DELTA2 = 0.0025
MESH = pl.DeviceIdType.MESH
BF = jnp.bfloat16
F32 = jnp.float32
TN = (((0,), (1,)), ((), ()))
TT = (((0,), (0,)), ((), ()))
NT = (((1,), (1,)), ((), ()))
YS, ZS, XS, SUBS = 4, 16, 2, 4


def rows_of(x):
    return lax.broadcasted_iota(jnp.int32, x.shape, 0)


def low_half(shape):
    return lax.broadcasted_iota(jnp.int32, shape, len(shape) - 1) < 64


def split2(x):
    high = x.astype(BF)
    return high, (x - high.astype(F32)).astype(BF)


def stacked(x):
    high = x.astype(BF).astype(F32)
    return jnp.concatenate([high, x - high], axis=0).astype(BF)


def split3(x):
    first = x.astype(BF).astype(F32)
    rest = x - first
    second = rest.astype(BF).astype(F32)
    return first, second, (rest - second).astype(BF).astype(F32)


def centred(rows):
    c = [r - 0.5 for r in rows]
    return c + [c[0] * c[0] + c[1] * c[1] + c[2] * c[2] + 0.5 * DELTA2]


def doubled(s):
    return jnp.concatenate([s, s], axis=1)


def source_rows(p8):
    p1, p2, p3 = split3(p8)
    norm = (rows_of(p8) & 3) == 3
    ones = jnp.where(norm, 1.0, p1)
    return jnp.concatenate([p1, p2, p3, ones, jnp.where(norm, 1.0, p2), ones], axis=0).astype(BF)


def target_rows(p8, first_half):
    p1, p2, p3 = split3(p8)
    row = rows_of(p8)
    norm = (row & 3) == 3
    active = ((row < 4) if first_half else (row >= 4)).astype(F32)
    lead = jnp.where(norm, 1.0, -2.0 * p1) * active
    return jnp.concatenate(
        [
            lead,
            lead,
            lead,
            jnp.where(norm, p1, -2.0 * p2) * active,
            jnp.where(norm, p2, -2.0 * p2) * active,
            jnp.where(norm, p3, -2.0 * p3) * active,
        ],
        axis=0,
    )


def split_dot(two, matrix, dims):
    high, low = split2(matrix)
    out = lax.dot_general(two, high, dims, preferred_element_type=F32) + lax.dot_general(
        two, low, dims, preferred_element_type=F32
    )
    half = out.shape[0] // 2
    return out[:half] + out[half:]


NN = (((1,), (0,)), ((), ()))
LP = 4


def body(
    near_list, far_list, mid_list, root_list,
    points, charges, leaf_skel, mid_skel, root_skel, leaf_transfer, mid_transfer,
    out,
    win, cwin, mids, roots, rpart, yroots, src, chg, cof, fld, mtw, msrc, mcof, rsrc, rcof, rsk,
    send, recv,
):
    leaf, sub = lax.axis_index("leaf"), lax.axis_index("sub")
    leaves = charges.shape[0]
    my_mids = mid_transfer.shape[0]
    window = 3 * leaves
    group = SUBS * my_mids
    flat = leaf * SUBS + sub
    start = (flat - 1) * leaves
    total = XS * ZS * YS * SUBS
    rank_scale = 1.0 / leaf_transfer.shape[1]
    leaf_scale = 1.0 / math.sqrt(charges.shape[2])
    x, z, y = leaf // (ZS * YS), (leaf // YS) % ZS, leaf % YS
    right, left = (flat + 1) % total, (flat + total - 1) % total
    right_id, left_id = (right // SUBS, right % SUBS), (left // SUBS, left % SUBS)
    sub_ids = [(leaf, (sub + k) % SUBS) for k in range(1, SUBS)]
    y_ids = [(leaf - y + (y + k) % YS, sub) for k in range(1, YS)]
    z_ids = [((x * ZS + (z + k) % ZS) * YS + y, sub) for k in range(1, ZS)]
    x_id = (((1 - x) * ZS + z) * YS + y, sub)

    barrier = pltpu.get_barrier_semaphore()
    partners = [right_id, left_id] + sub_ids + y_ids + z_ids + [x_id]
    for partner in partners:
        pl.semaphore_signal(barrier, inc=1, device_id=partner, device_id_type=MESH)

    def copy(slot, source, target_ref, target):
        return pltpu.make_async_remote_copy(
            src_ref=source, dst_ref=target_ref, send_sem=send.at[slot], recv_sem=recv.at[slot],
            device_id=target, device_id_type=MESH,
        )

    def halo(slot, ref):
        own = ref.at[pl.ds(leaves, leaves)]
        return [
            copy(slot, own, ref.at[pl.ds(0, leaves)], right_id),
            copy(slot + 1, own, ref.at[pl.ds(2 * leaves, leaves)], left_id),
        ]

    half = low_half((8, 128))
    lane48 = low_half((48, 128))
    lane16 = low_half((16, 128))
    zero = jnp.zeros((16, 128), BF)

    own_rows = pl.ds(leaves, leaves)
    for r, value in enumerate(centred([points[c] for c in range(3)])):
        win[own_rows, r, :] = value
    for r, value in enumerate(centred([doubled(leaf_skel[c]) for c in range(3)])):
        win[own_rows, 4 + r, :] = value
    win[own_rows, pl.ds(8, 8), :] = charges[...]
    own_mid_rows = pl.ds(sub * my_mids, my_mids)
    for r, value in enumerate(centred([doubled(mid_skel[c]) for c in range(3)])):
        mids[own_mid_rows, 8 + r, :] = value
        mids[own_mid_rows, 12 + r, :] = value

    def one_leaf(i, carry):
        w = win[leaves + i]
        rows = source_rows(w[:8])
        two = stacked(w[8:])
        src[leaves + i] = rows
        chg[leaves + i] = two
        skel = jnp.concatenate([w[4:8], w[4:8]], axis=0)
        tgt = target_rows(skel, True).astype(BF)
        d2 = lax.dot_general(rows, tgt, TT, preferred_element_type=F32)
        coeff = split_dot(two, lax.rsqrt(d2), NN) * leaf_scale
        cwin[leaves + i] = coeff
        cof[leaves + i] = stacked(coeff)
        return carry

    lax.fori_loop(0, leaves // 2, one_leaf, 0, unroll=4)
    pl.semaphore_wait(barrier, len(partners))
    points_halo = halo(6, win)
    for c in points_halo:
        c.start()
    lax.fori_loop(leaves // 2, leaves, one_leaf, 0, unroll=4)
    coeff_halo = halo(8, cwin)
    for c in coeff_halo:
        c.start()

    def lifted(low_child, high_child, pair):
        both = jnp.where(half, low_child, high_child)
        return split_dot(stacked(both), doubled(pair.reshape(128, 64)), NN)

    mid_coeffs = []
    for m in range(my_mids):
        acc = jnp.zeros((8, 128), F32)
        for k in range(0, 8, 2):
            c = m * 8 + k
            acc += lifted(cwin[leaves + c], cwin[leaves + c + 1], leaf_transfer[c : c + 2])
        mid_coeffs.append(acc)
        mids[sub * my_mids + m, pl.ds(0, 8), :] = acc
    partial = jnp.zeros((8, 128), F32)
    for m in range(0, my_mids, 2):
        partial += lifted(mid_coeffs[m], mid_coeffs[m + 1], mid_transfer[m : m + 2])
    rpart[sub] = partial
    own_mids = mids.at[own_mid_rows]
    mid_copies = [copy(3 + k, own_mids, own_mids, sub_ids[k]) for k in range(3)]
    sums = [copy(k, rpart.at[sub], rpart.at[sub], sub_ids[k]) for k in range(3)]
    for c in mid_copies + sums:
        c.start()

    src[window] = src[leaves]
    chg[window] = zero
    cof[window] = zero
    for c in range(3):
        rsk[c] = doubled(root_skel[c].T)

    for c in points_halo:
        c.wait()

    def build(j, carry):
        for k in (j, 2 * leaves + j):
            w = win[k]
            src[k] = source_rows(w[:8])
            chg[k] = stacked(w[8:])
        return carry

    lax.fori_loop(0, leaves, build, 0, unroll=2)

    def place(j, first, empty):
        return jnp.where(j >= 0, jnp.clip(j - first, 0, empty - 1), empty)

    def near_leaves(t, carry):
        ids = [t * LP + p for p in range(LP)]
        tgts = [target_rows(win[leaves + i][:8], True).T.astype(BF) for i in ids]
        accs = [jnp.zeros((16, 128), F32)] * LP
        count = near_list.shape[1]
        for g in range(0, count, 2):
            for p, i in enumerate(ids):
                js = [place(near_list[i, k], start, window) for k in range(g, min(g + 2, count))]
                s = jnp.concatenate([src[j] for j in js], axis=1)
                q = jnp.concatenate([chg[j] for j in js], axis=1)
                d2 = lax.dot_general(s, tgts[p], TN, preferred_element_type=F32)
                high, low = split2(lax.rsqrt(d2))
                accs[p] += jnp.dot(q, high, preferred_element_type=F32) + jnp.dot(
                    q, low, preferred_element_type=F32
                )
        for p, i in enumerate(ids):
            out[i] = (accs[p][:8] + accs[p][8:]) * (1.0 / 128.0)
        return carry

    for c in sums:
        c.wait()
    yroots[y] = (rpart[0] + rpart[1]) + (rpart[2] + rpart[3])
    stage = [copy(10 + k, yroots.at[y], yroots.at[y], y_ids[k]) for k in range(YS - 1)]
    for c in stage:
        c.start()
    lax.fori_loop(0, 1, near_leaves, 0)
    for c in stage:
        c.wait()
    roots[x, z, 0] = jnp.where(half, yroots[0], yroots[1])
    roots[x, z, 1] = jnp.where(half, yroots[2], yroots[3])
    own = roots.at[x, z]
    stage = [copy(13 + k, own, own, z_ids[k]) for k in range(ZS - 1)]
    for c in stage:
        c.start()
    lax.fori_loop(1, 4, near_leaves, 0)
    for c in stage:
        c.wait()
    last = copy(28, roots.at[x], roots.at[x], x_id)
    last.start()
    lax.fori_loop(4, leaves // LP, near_leaves, 0)

    for c in coeff_halo + mid_copies:
        c.wait()

    def build_coeffs(j, carry):
        for k in (j, 2 * leaves + j):
            cof[k] = stacked(cwin[k])
        return carry

    lax.fori_loop(0, leaves, build_coeffs, 0, unroll=4)
    for j in range(group):
        w = mids[j]
        msrc[j] = source_rows(w[8:])
        mcof[j] = stacked(w[:8])
    msrc[group] = msrc[0]
    mcof[group] = zero

    def far_targets(p8):
        rows = target_rows(p8, False)
        low = low_half(rows.shape)
        pair = jnp.concatenate([jnp.where(low, rows, 0.0), jnp.where(low, 0.0, rows)], axis=0)
        return pair.T.astype(BF)

    def quad(js, table, coeffs, tgt):
        a, b, c, d = js
        s = jnp.concatenate(
            [jnp.where(lane48, table[a], table[c]), jnp.where(lane48, table[b], table[d])], axis=0
        )
        q = jnp.concatenate(
            [jnp.where(lane16, coeffs[a], coeffs[c]), jnp.where(lane16, coeffs[b], coeffs[d])],
            axis=0,
        )
        high, low = split2(lax.rsqrt(lax.dot_general(s, tgt, TN, preferred_element_type=F32)))
        return jnp.dot(q, high, preferred_element_type=F32) + jnp.dot(
            q, low, preferred_element_type=F32
        )

    def field(acc):
        s = jnp.where(half, acc[0:8] + acc[8:16], acc[16:24] + acc[24:32])
        return (s + pltpu.roll(s, 64, 1)) * rank_scale

    def far_leaves(t, carry):
        ids = [t * LP + p for p in range(LP)]
        tgts = [far_targets(win[leaves + i][:8]) for i in ids]
        accs = [jnp.zeros((32, 128), F32)] * LP
        for g in range(0, far_list.shape[0], 4):
            for p, i in enumerate(ids):
                js = [place(far_list[g + k, i], start, window) for k in range(4)]
                accs[p] += quad(js, src, cof, tgts[p])
        for p, i in enumerate(ids):
            fld[i] = field(accs[p])
        return carry

    lax.fori_loop(0, leaves // LP, far_leaves, 0)
    mid_fields = []
    for m in range(my_mids):
        js = [place(mid_list[m, k], leaf * group, group) for k in range(mid_list.shape[1])]
        js += [group] * (8 - len(js))
        tgt = far_targets(mids[sub * my_mids + m, pl.ds(8, 8), :])
        mid_fields.append(
            field(quad(js[:4], msrc, mcof, tgt) + quad(js[4:], msrc, mcof, tgt))
        )

    def root_p8(r):
        rows = centred([rsk[c, pl.ds(r, 1), :] for c in range(3)])
        return jnp.concatenate(rows + rows, axis=0)

    last.wait()
    slots = root_list.shape[1]
    for k in range(slots):
        r = root_list[0, k]
        present = (r >= 0).astype(F32)
        r = jnp.maximum(r, 0)
        tile = roots[r // (2 * ZS * 2), (r // YS) % ZS, (r // 2) % 2]
        mine = (lax.broadcasted_iota(jnp.int32, (8, 128), 1) // 64) == (r % 2)
        coeff = jnp.where(mine, tile, pltpu.roll(tile, 64, 1))
        rsrc[k] = source_rows(root_p8(r))
        rcof[k] = stacked(coeff * present)
    for k in range(slots, 8):
        rsrc[k] = rsrc[0]
        rcof[k] = zero
    tgt = far_targets(root_p8(leaf))
    acc = quad((0, 1, 2, 3), rsrc, rcof, tgt) + quad((4, 5, 6, 7), rsrc, rcof, tgt)
    root_two = stacked(field(acc))[:, :64]
    for m in range(my_mids):
        value = mid_fields[m][:, :64] + split_dot(root_two, mid_transfer[m], NT)
        mtw[m] = stacked(value)

    def finish(t, carry):
        for p in range(LP):
            i = t * LP + p
            lowered = split_dot(mtw[i // 8], leaf_transfer[i], NT)
            two = stacked((fld[i][:, :64] + lowered) * leaf_scale)
            w = win[leaves + i]
            own = jnp.concatenate([w[:4], w[:4]], axis=0)
            basis = target_rows(own, False).T.astype(BF)
            d2 = lax.dot_general(src[leaves + i][:, :64], basis, TN, preferred_element_type=F32)
            out[i] += split_dot(two, lax.rsqrt(d2), NN)
        return carry

    lax.fori_loop(0, leaves // LP, finish, 0)


def local(
    points, charges, leaf_skel, mid_skel, root_skel, leaf_transfer, mid_transfer,
    near_list, far_list, mid_list, root_list,
):
    leaves = points.shape[0]
    mids = mid_skel.shape[0]
    window = 3 * leaves + 1
    group = SUBS * mids + 1
    vmem = pl.BlockSpec(memory_space=pltpu.VMEM)
    smem = pl.BlockSpec(memory_space=pltpu.SMEM)
    return pl.pallas_call(
        body,
        name="h2_product",
        out_shape=jax.ShapeDtypeStruct((leaves, 8, 128), F32),
        in_specs=[smem] * 4 + [vmem] * 7,
        out_specs=vmem,
        scratch_shapes=[
            pltpu.VMEM((3 * leaves, 16, 128), F32),
            pltpu.VMEM((3 * leaves, 8, 128), F32),
            pltpu.VMEM((SUBS * mids, 16, 128), F32),
            pltpu.VMEM((XS, ZS, YS // 2, 8, 128), F32),
            pltpu.VMEM((SUBS, 8, 128), F32),
            pltpu.VMEM((YS, 8, 128), F32),
            pltpu.VMEM((window, 48, 128), BF),
            pltpu.VMEM((window, 16, 128), BF),
            pltpu.VMEM((window, 16, 128), BF),
            pltpu.VMEM((leaves, 8, 128), F32),
            pltpu.VMEM((mids, 16, 64), BF),
            pltpu.VMEM((group, 48, 128), BF),
            pltpu.VMEM((group, 16, 128), BF),
            pltpu.VMEM((8, 48, 128), BF),
            pltpu.VMEM((8, 16, 128), BF),
            pltpu.VMEM((3, XS * ZS * YS, 128), F32),
            pltpu.SemaphoreType.DMA((29,)),
            pltpu.SemaphoreType.DMA((29,)),
        ],
        compiler_params=pltpu.CompilerParams(collective_id=0, has_side_effects=True),
    )(
        near_list, far_list.T, mid_list, root_list,
        points.transpose(1, 0, 2), charges, leaf_skel.transpose(1, 0, 2),
        mid_skel.transpose(1, 0, 2), root_skel.transpose(1, 2, 0), leaf_transfer, mid_transfer,
    )


def solution(mesh):
    both = P(("leaf", "sub"), None, None)
    lists = P(("leaf", "sub"), None)
    in_specs = (both, both, both, both, P(), both, both, lists, lists, lists, P("leaf", None))
    return jax.shard_map(local, mesh=mesh, in_specs=in_specs, out_specs=both, check_vma=False)
```

time: 90.5 us -> 72.7 us (0.80)
  Pallas kernels: 85.9 us -> 71 us
  local copies, waits for them, and re-layouts: 4.29 us -> 1.57 us
    pallas_call x2 -> x1, Pallas kernels: 85.9 us -> 71 us  [local(): pl.pallas_call(body, name='h2_product', out_shape=jax.ShapeDtypeStruct((l...]
    unnamed x13 -> x1, local copies, waits for them, and re-layouts: 4.29 us -> 1.57 us
where the time goes in v2:
time: 72.7 us; the launch traced here: 72.6 us
  Pallas kernels  71 us (98%)
  local copies, waits for them, and re-layouts  1.57 us (2%)
    pallas_call x1, Pallas kernels, local(): pl.pallas_call(body, name='h2_product', out_shape=jax.ShapeDtypeStruct((l...  71 us
    unnamed x1, local copies, waits for them, and re-layouts  1.57 us

profile of v2, /device:TPU:8, one launch (start us, length us, event | category | flops | bytes accessed | tf_op | source)
XLA Modules:
  0.0 72.6 jit_solution(187383861988845911)
XLA Ops:
  0.0 71.0 %h2_product.1 = f32[32,8,128]{2,1,0:T(8,128)} custom-call(s32[32,27]{1,0:T(8,128)} %near_list.1, s32[20,32]{1,0:T(8,128)} %bitcast.8, s32[4,6]{1,0:T(4,128)} %mid_list.1, s32[1,6]{1,0:T(1,128)} %root_list.1, f32[3,32,128]{2,1,0:T(8,128)} %bitcast.6, f32[32,8,128]{2,1,0:T(8,128)} %charges.1, f32[3,32,64]{2,1,0:T(8,128)} %bitcast.7, f32[3,4,64]{2,1,0:T(4,128)} %bitcast.9, ...), custom_call_target="tpu_custom_call" | custom-call | tf_op jit(solution)/shard_map/h2_product/pallas_call | solution.py:373
  71.0 1.6 %copy.13 = f32[32,8,128]{2,1,0:T(8,128)} copy(f32[32,8,128]{2,1,0:T(8,128)} %h2_product.1) | data formatting | bytes 262144

commit v3 on v2

--- a/solution.py
+++ b/solution.py
@@ -170,10 +170,6 @@
     for c in points_halo:
         c.start()
     lax.fori_loop(leaves // 2, leaves, one_leaf, 0, unroll=4)
-    coeff_halo = halo(8, cwin)
-    for c in coeff_halo:
-        c.start()
-
     def lifted(low_child, high_child, pair):
         both = jnp.where(half, low_child, high_child)
         return split_dot(stacked(both), doubled(pair.reshape(128, 64)), NN)
@@ -193,7 +189,7 @@
     own_mids = mids.at[own_mid_rows]
     mid_copies = [copy(3 + k, own_mids, own_mids, sub_ids[k]) for k in range(3)]
     sums = [copy(k, rpart.at[sub], rpart.at[sub], sub_ids[k]) for k in range(3)]
-    for c in mid_copies + sums:
+    for c in sums + mid_copies:
         c.start()
 
     src[window] = src[leaves]
@@ -236,13 +232,14 @@
             out[i] = (accs[p][:8] + accs[p][8:]) * (1.0 / 128.0)
         return carry
 
+    lax.fori_loop(0, 1, near_leaves, 0)
     for c in sums:
         c.wait()
     yroots[y] = (rpart[0] + rpart[1]) + (rpart[2] + rpart[3])
     stage = [copy(10 + k, yroots.at[y], yroots.at[y], y_ids[k]) for k in range(YS - 1)]
     for c in stage:
         c.start()
-    lax.fori_loop(0, 1, near_leaves, 0)
+    lax.fori_loop(1, 2, near_leaves, 0)
     for c in stage:
         c.wait()
     roots[x, z, 0] = jnp.where(half, yroots[0], yroots[1])
@@ -251,12 +248,15 @@
     stage = [copy(13 + k, own, own, z_ids[k]) for k in range(ZS - 1)]
     for c in stage:
         c.start()
-    lax.fori_loop(1, 4, near_leaves, 0)
+    coeff_halo = halo(8, cwin)
+    for c in coeff_halo:
+        c.start()
+    lax.fori_loop(2, 6, near_leaves, 0)
     for c in stage:
         c.wait()
     last = copy(28, roots.at[x], roots.at[x], x_id)
     last.start()
-    lax.fori_loop(4, leaves // LP, near_leaves, 0)
+    lax.fori_loop(6, leaves // LP, near_leaves, 0)
 
     for c in coeff_halo + mid_copies:
         c.wait()

time: 72.7 us -> 67 us (0.922)
  the two profiles are of different devices: /device:TPU:8 before, /device:TPU:1 now
where the time goes in v3:
time: 67 us; the launch traced here: 66.8 us
  Pallas kernels  65.3 us (97%)
  local copies, waits for them, and re-layouts  1.57 us (2%)
    pallas_call x1, Pallas kernels, local(): pl.pallas_call(body, name='h2_product', out_shape=jax.ShapeDtypeStruct((l...  65.3 us
    unnamed x1, local copies, waits for them, and re-layouts  1.57 us

profile of v3, /device:TPU:1, one launch (start us, length us, event | category | flops | bytes accessed | tf_op | source)
XLA Modules:
  0.0 66.8 jit_solution(10180079629401116612)
XLA Ops:
  0.0 65.3 %h2_product.1 = f32[32,8,128]{2,1,0:T(8,128)} custom-call(s32[32,27]{1,0:T(8,128)} %near_list.1, s32[20,32]{1,0:T(8,128)} %bitcast.8, s32[4,6]{1,0:T(4,128)} %mid_list.1, s32[1,6]{1,0:T(1,128)} %root_list.1, f32[3,32,128]{2,1,0:T(8,128)} %bitcast.6, f32[32,8,128]{2,1,0:T(8,128)} %charges.1, f32[3,32,64]{2,1,0:T(8,128)} %bitcast.7, f32[3,4,64]{2,1,0:T(4,128)} %bitcast.9, ...), custom_call_target="tpu_custom_call" | custom-call | tf_op jit(solution)/shard_map/h2_product/pallas_call | solution.py:373
  65.3 1.6 %copy.13 = f32[32,8,128]{2,1,0:T(8,128)} copy(f32[32,8,128]{2,1,0:T(8,128)} %h2_product.1) | data formatting | bytes 262144

commit v4 on v3

--- a/solution.py
+++ b/solution.py
@@ -150,26 +150,32 @@
         mids[own_mid_rows, 8 + r, :] = value
         mids[own_mid_rows, 12 + r, :] = value
 
-    def one_leaf(i, carry):
-        w = win[leaves + i]
-        rows = source_rows(w[:8])
-        two = stacked(w[8:])
-        src[leaves + i] = rows
-        chg[leaves + i] = two
-        skel = jnp.concatenate([w[4:8], w[4:8]], axis=0)
-        tgt = target_rows(skel, True).astype(BF)
-        d2 = lax.dot_general(rows, tgt, TT, preferred_element_type=F32)
-        coeff = split_dot(two, lax.rsqrt(d2), NN) * leaf_scale
-        cwin[leaves + i] = coeff
-        cof[leaves + i] = stacked(coeff)
-        return carry
-
-    lax.fori_loop(0, leaves // 2, one_leaf, 0, unroll=4)
+    def some_leaves(t, carry):
+        ids = [leaves + t * LP + p for p in range(LP)]
+        ws = [win[i] for i in ids]
+        rows = [source_rows(w[:8]) for w in ws]
+        twos = [stacked(w[8:]) for w in ws]
+        tgts = [
+            target_rows(jnp.concatenate([w[4:8], w[4:8]], axis=0), True).astype(BF) for w in ws
+        ]
+        d2 = [
+            lax.dot_general(r, g, TT, preferred_element_type=F32) for r, g in zip(rows, tgts)
+        ]
+        basis = [lax.rsqrt(d) for d in d2]
+        coeffs = [split_dot(two, g, NN) * leaf_scale for two, g in zip(twos, basis)]
+        for i, r, two, coeff in zip(ids, rows, twos, coeffs):
+            src[i] = r
+            chg[i] = two
+            cwin[i] = coeff
+            cof[i] = stacked(coeff)
+        return carry
+
+    lax.fori_loop(0, leaves // (2 * LP), some_leaves, 0)
     pl.semaphore_wait(barrier, len(partners))
     points_halo = halo(6, win)
     for c in points_halo:
         c.start()
-    lax.fori_loop(leaves // 2, leaves, one_leaf, 0, unroll=4)
+    lax.fori_loop(leaves // (2 * LP), leaves // LP, some_leaves, 0)
     def lifted(low_child, high_child, pair):
         both = jnp.where(half, low_child, high_child)
         return split_dot(stacked(both), doubled(pair.reshape(128, 64)), NN)
@@ -346,15 +352,21 @@
         mtw[m] = stacked(value)
 
     def finish(t, carry):
-        for p in range(LP):
-            i = t * LP + p
-            lowered = split_dot(mtw[i // 8], leaf_transfer[i], NT)
-            two = stacked((fld[i][:, :64] + lowered) * leaf_scale)
-            w = win[leaves + i]
-            own = jnp.concatenate([w[:4], w[:4]], axis=0)
-            basis = target_rows(own, False).T.astype(BF)
-            d2 = lax.dot_general(src[leaves + i][:, :64], basis, TN, preferred_element_type=F32)
-            out[i] += split_dot(two, lax.rsqrt(d2), NN)
+        ids = [t * LP + p for p in range(LP)]
+        rows = [win[leaves + i][:4] for i in ids]
+        tgts = [
+            target_rows(jnp.concatenate([w, w], axis=0), False).T.astype(BF) for w in rows
+        ]
+        lowered = [split_dot(mtw[i // 8], leaf_transfer[i], NT) for i in ids]
+        d2 = [
+            lax.dot_general(src[leaves + i][:, :64], g, TN, preferred_element_type=F32)
+            for i, g in zip(ids, tgts)
+        ]
+        basis = [lax.rsqrt(d) for d in d2]
+        twos = [stacked((fld[i][:, :64] + w) * leaf_scale) for i, w in zip(ids, lowered)]
+        terms = [split_dot(two, g, NN) for two, g in zip(twos, basis)]
+        for i, term in zip(ids, terms):
+            out[i] += term
         return carry
 
     lax.fori_loop(0, leaves // LP, finish, 0)

time: 67 us -> 63.2 us (0.943)
  Pallas kernels: 65.3 us -> 61.5 us
    pallas_call x1, Pallas kernels: 65.3 us -> 61.5 us  [local(): pl.pallas_call(body, name='h2_product', out_shape=jax.ShapeDtypeStruct((l...]
where the time goes in v4:
time: 63.2 us; the launch traced here: 63 us
  Pallas kernels  61.5 us (97%)
  local copies, waits for them, and re-layouts  1.57 us (2%)
    pallas_call x1, Pallas kernels, local(): pl.pallas_call(body, name='h2_product', out_shape=jax.ShapeDtypeStruct((l...  61.5 us
    unnamed x1, local copies, waits for them, and re-layouts  1.57 us

profile of v4, /device:TPU:1, one launch (start us, length us, event | category | flops | bytes accessed | tf_op | source)
XLA Modules:
  0.0 63.0 jit_solution(12510838244902613741)
XLA Ops:
  0.0 61.5 %h2_product.1 = f32[32,8,128]{2,1,0:T(8,128)} custom-call(s32[32,27]{1,0:T(8,128)} %near_list.1, s32[20,32]{1,0:T(8,128)} %bitcast.8, s32[4,6]{1,0:T(4,128)} %mid_list.1, s32[1,6]{1,0:T(1,128)} %root_list.1, f32[3,32,128]{2,1,0:T(8,128)} %bitcast.6, f32[32,8,128]{2,1,0:T(8,128)} %charges.1, f32[3,32,64]{2,1,0:T(8,128)} %bitcast.7, f32[3,4,64]{2,1,0:T(4,128)} %bitcast.9, ...), custom_call_target="tpu_custom_call" | custom-call | tf_op jit(solution)/shard_map/h2_product/pallas_call | solution.py:385
  61.5 1.6 %copy.13 = f32[32,8,128]{2,1,0:T(8,128)} copy(f32[32,8,128]{2,1,0:T(8,128)} %h2_product.1) | data formatting | bytes 262144
